TPU v7x, 256 devices: a whole 4x4x8 slice. The times are simulated.
256 devices in a mesh: row: 16 (over y, z_lo), col: 16 (over x, z_hi, core).
Axes of the slice: x: 4, y: 4, z: 8 (z_hi: 2, z_lo: 4; z = z_hi * 4 + z_lo), core: 2. Of those that a mesh axis runs over, the one named last changes fastest.
Arguments:
- features: float32 [65536, 128], P(('col', 'row')), may hold values from -6 to 6
- weight: float32 [128, 128], replicated, may hold values from -4 to 4
- bias_vector: float32 [128], replicated, may hold values from -4 to 4
- out_grad: float32 [65536, 128], P(('row', 'col')), may hold values from -6 to 6
- adj_tiles: int32 [16, 16, 128, 128, 128], P('row', 'col'), may hold values 0 or 1
- tile_slots: int32 [16, 16, 128], P('row', 'col'), may hold values from 0 to 1023, as said below
- tile_counts: int32 [16, 16], P('row', 'col'), may hold values from 17 to 128, as said below
Outputs:
- activated: float32 [65536, 128], P(('row', 'col'))
- feature_grad: float32 [65536, 128], P(('col', 'row'))
- weight_grad: float32 [128, 128], replicated
- bias_grad: float32 [128], replicated
Inputs may be any that keep to these rules, and one draw needn't show every extreme that they name: `tile_slots`: each block's slots name distinct positions r * 32 + c of its 32 x 32 tiles. Some block is full in every draw; slots from tile_counts on are ignored.
All inputs are finite; a program needn't handle non-finite values. No bound on the sum of `adj_tiles` on one device may be relied on, other than what follows from the above.
Results may differ from a plain program's by a relative error of at most 0.0003.
Values sent between devices are 32-bit elements; how exact they have to be, the bound alone decides.
A program may use at most 128 MiB of HBM per device.

v0:
```python
import jax
import jax.numpy as jnp
from jax import lax
from jax.sharding import PartitionSpec as P

TILE = 128


def dense_step(aggregated, weight, bias_vector, cotangent):
    preact = jnp.dot(aggregated, weight, precision=lax.Precision.HIGHEST) + bias_vector
    logistic = jax.nn.sigmoid(preact)
    activated = preact * logistic
    pre_grad = cotangent * logistic * (1.0 + preact * (1.0 - logistic))
    weight_part = jnp.dot(aggregated.T, pre_grad, precision=lax.Precision.HIGHEST)
    bias_part = jnp.sum(pre_grad, axis=0)
    back_rows = jnp.dot(pre_grad, weight.T, precision=lax.Precision.HIGHEST)
    return (activated, weight_part, bias_part, back_rows)


def local(features, weight, bias_vector, out_grad, adj_tiles, tile_slots, tile_counts):
    row_count = lax.axis_size("row")
    col_count = lax.axis_size("col")
    node_rows = features.shape[0]
    width = features.shape[1]
    tile_rows = node_rows * col_count // TILE
    tile_cols = node_rows * row_count // TILE
    adjacency = adj_tiles[0, 0].astype(jnp.float32)
    slots = tile_slots[0, 0]
    slot_total = slots.shape[0]
    live_mask = (jnp.arange(slot_total) < tile_counts[0, 0]).astype(jnp.float32)
    tile_row = slots // tile_cols
    tile_col = slots % tile_cols
    row_select = (tile_row[:, None] == jnp.arange(tile_rows)[None, :]).astype(
        jnp.float32
    ) * live_mask[:, None]
    col_select = (tile_col[:, None] == jnp.arange(tile_cols)[None, :]).astype(
        jnp.float32
    ) * live_mask[:, None]
    dst_partial = jnp.dot(
        row_select.T, jnp.sum(adjacency, axis=2), precision=lax.Precision.HIGHEST
    ).reshape(-1)
    src_partial = jnp.dot(
        col_select.T, jnp.sum(adjacency, axis=1), precision=lax.Precision.HIGHEST
    ).reshape(-1)
    src_scale = lax.rsqrt(
        1.0 + lax.psum_scatter(src_partial, "row", scatter_dimension=0, tiled=True)
    )
    scaled = features * src_scale[:, None]
    gathered = lax.all_gather(scaled, "row", axis=0, tiled=True)
    taken = jnp.take(gathered.reshape(tile_cols, TILE, width), tile_col, axis=0)
    product = jnp.einsum(
        "kab,kbh->kah",
        adjacency,
        taken,
        precision=lax.Precision.HIGHEST,
        preferred_element_type=jnp.float32,
    )
    partial_value = jnp.einsum(
        "kr,kah->rah",
        row_select,
        product,
        precision=lax.Precision.HIGHEST,
        preferred_element_type=jnp.float32,
    ).reshape(tile_rows * TILE, width)
    dst_scale = lax.rsqrt(
        1.0 + lax.psum_scatter(dst_partial, "col", scatter_dimension=0, tiled=True)
    )
    aggregated = (
        lax.psum_scatter(partial_value, "col", scatter_dimension=0, tiled=True) * dst_scale[:, None]
    )
    activated, weight_part, bias_part, back_rows = dense_step(
        aggregated, weight, bias_vector, out_grad
    )
    weight_grad, bias_grad = lax.psum((weight_part, bias_part), ("row", "col"))
    row_grads = lax.all_gather(back_rows * dst_scale[:, None], "col", axis=0, tiled=True)
    taken_back = jnp.take(row_grads.reshape(tile_rows, TILE, width), tile_row, axis=0)
    product_back = jnp.einsum(
        "kab,kah->kbh",
        adjacency,
        taken_back,
        precision=lax.Precision.HIGHEST,
        preferred_element_type=jnp.float32,
    )
    partial_back = jnp.einsum(
        "kc,kbh->cbh",
        col_select,
        product_back,
        precision=lax.Precision.HIGHEST,
        preferred_element_type=jnp.float32,
    ).reshape(tile_cols * TILE, width)
    feature_grad = (
        lax.psum_scatter(partial_back, "row", scatter_dimension=0, tiled=True) * src_scale[:, None]
    )
    return (activated, feature_grad, weight_grad, bias_grad)


def solution(mesh):
    return jax.shard_map(
        local,
        mesh=mesh,
        in_specs=(
            P(("col", "row"), None),
            P(),
            P(),
            P(("row", "col"), None),
            P("row", "col", None, None, None),
            P("row", "col", None),
            P("row", "col"),
        ),
        out_specs=(P(("row", "col"), None), P(("col", "row"), None), P(), P()),
        check_vma=False,
    )
```

profile of v0, /device:TPU:1, one launch (start us, length us, event | category | flops | bytes accessed | tf_op | source)
XLA Modules:
  0.0 764.2 jit_solution(688655162839533169)
XLA Ops:
  7.9 1.3 dynamic-slice
  9.9 5.7 convert_reduce_fusion
  15.8 68.3 %all-reduce = f32[4096]{0:T(1024)S(1)} all-reduce(f32[4096]{0:T(1024)S(1)} %convolution_bitcast_fusion.1), channel_id=2, replica_groups=mesh['row'=16,'col'=16] {'row'}, use_global_device_ids=true, to_apply=%region_1.2.clone | all-reduce | flops 4096 | bytes 32768
  85.1 89.2 %all-gather.3.cloned.1.call-done = f32[4096,128]{1,0:T(8,128)} async-done(((f32[256,128]{1,0:T(8,128)}), f32[4096,128]{1,0:T(8,128)}) %all-gather.3.cloned.1.call-update) | async-done | bytes 2097168 | tf_op jit(solution)/shard_map/all_gather | solution.py:49
  174.3 5.9 gather_fusion
  180.1 21.5 %fusion.12 = f32[128,128,128]{1,2,0:T(8,128)} fusion(s32[1,1,128,128,128]{4,3,2,1,0:T(8,128)} %param.13, f32[128,128,128]{2,1,0:T(8,128)} %gather_fusion, pred[128]{0:T(512)(128)(4,1)S(1)} %get-tuple-element.14), kind=kOutput, calls=%fused_computation.16 | convolution fusion | flops 3225419776 | bytes 25165952 | tf_op jit(solution)/shard_map/kab,kbh->kah/dot_general | solution.py:51
  201.7 9.3 %copy.18 = f32[128,128,128]{2,0,1:T(8,128)} copy(f32[128,128,128]{1,2,0:T(8,128)} %fusion.12) | data formatting | bytes 16777216 | tf_op jit(solution)/shard_map/kab,kbh->kah/dot_general | solution.py:51
  211.0 6.8 fusion.30
  217.7 2.6 copy.19
  221.8 87.6 %all-reduce.1 = f32[4096]{0:T(1024)S(1)} all-reduce(f32[4096]{0:T(1024)S(1)} %convolution_bitcast_fusion), channel_id=4, replica_groups=mesh['row'=16,'col'=16] {'col'}, use_global_device_ids=true, to_apply=%region_4.6.clone | all-reduce | flops 4096 | bytes 32768
  309.5 4.8 reduce-scatter.3.cloned.1.call-done
  314.3 1.9 fusion.52
  316.2 0.9 convolution_multiply_fusion
  317.2 62.5 %all-gather.5.cloned.1.call-done = f32[4096,128]{1,0:T(8,128)} async-done(((f32[256,128]{1,0:T(8,128)}), f32[4096,128]{1,0:T(8,128)}) %all-gather.5.cloned.1.call-update) | async-done | bytes 2097168 | tf_op jit(solution)/shard_map/all_gather | solution.py:75
  379.7 5.9 gather_fusion.1
  385.6 19.7 %fusion.17 = f32[128,128,128]{1,2,0:T(8,128)} fusion(s32[1,1,128,128,128]{4,3,2,1,0:T(8,128)} %param.13, f32[128,128,128]{2,1,0:T(8,128)} %gather_fusion.1, pred[128]{0:T(512)(128)(4,1)S(1)} %get-tuple-element.9), kind=kOutput, calls=%fused_computation.17 | convolution fusion | flops 3225419776 | bytes 25165952 | tf_op jit(solution)/shard_map/kab,kah->kbh/dot_general | solution.py:77
  405.3 9.3 %copy.21 = f32[128,128,128]{2,0,1:T(8,128)} copy(f32[128,128,128]{1,2,0:T(8,128)} %fusion.17) | data formatting | bytes 16777216 | tf_op jit(solution)/shard_map/kab,kah->kbh/dot_general | solution.py:77
  414.6 6.8 fusion.31
  421.4 2.6 copy.22
  424.0 76.6 %psum.15 = f32[128]{0:T(128)} all-reduce(f32[128]{0:T(128)S(1)} %get-tuple-element.7), channel_id=1, replica_groups=mesh['row'=16,'col'=16] {'row','col'}, use_global_device_ids=true, to_apply=%region_8.10 | all-reduce | flops 128 | bytes 1024 | tf_op jit(solution)/shard_map/psum | solution.py:74
  500.6 1.1 fusion.23
  501.8 1.7 broadcast_multiply_fusion
  503.4 252.8 %all-reduce.4.cloned.1.call-done = f32[128,128]{1,0:T(8,128)} async-done(((f32[128,128]{1,0:T(8,128)}), f32[128,128]{1,0:T(8,128)}) %all-reduce.4.cloned.1.call-update) | async-done | bytes 65552 | tf_op jit(solution)/shard_map/psum | solution.py:74
  756.2 1.5 copy.27
  (36 shorter events, 2.2 us)
Async XLA Ops:
  7.2 307.1 %copy-start = (f32[128,128]{1,0:T(8,128)S(1)}, f32[128,128]{1,0:T(8,128)}, u32[]{:S(2)}) copy-start(f32[128,128]{1,0:T(8,128)} %param.10) | copy-start | bytes 196612
  7.2 8.4 %copy-start.3 = (s32[1,1,128]{2,1,0:T(1,128)S(1)}, s32[1,1,128]{2,1,0:T(1,128)}, u32[]{:S(2)}) copy-start(s32[1,1,128]{2,1,0:T(1,128)} %param.14) | copy-start | bytes 1540
  7.2 77.0 %copy-start.1 = (f32[256,128]{1,0:T(8,128)S(1)}, f32[256,128]{1,0:T(8,128)}, u32[]{:S(2)}) copy-start(f32[256,128]{1,0:T(8,128)} %param.9) | copy-start | bytes 393220
  7.2 167.1 %all-gather.3.cloned.1.call-start = ((), (), s32[]{:S(2)}) async-start(), calls=%async_computation.2 | async-start | bytes 2228224 | tf_op jit(solution)/shard_map/all_gather | solution.py:49
  85.0 229.3 %reduce-scatter.3.cloned.1.call-start = ((), (), s32[]{:S(2)}) async-start(), calls=%async_computation.3 | async-start | bytes 2228224 | tf_op jit(solution)/shard_map/reduce_scatter | solution.py:69
  211.0 9.4 %copy-start.6 = (u32[256]{0:T(256)S(1)}, u32[256]{0:T(256)}, u32[]{:S(2)}) copy-start(u32[256]{0:T(256)} %constant.56) | copy-start | bytes 3076
  211.0 103.3 %copy-start.4 = (f32[256,128]{1,0:T(8,128)S(1)}, f32[256,128]{1,0:T(8,128)}, u32[]{:S(2)}) copy-start(f32[256,128]{1,0:T(8,128)} %param.12) | copy-start | bytes 393220
  211.0 103.3 %copy-start.5 = (f32[128]{0:T(128)S(1)}, f32[128]{0:T(128)}, u32[]{:S(2)}) copy-start(f32[128]{0:T(128)} %param.11) | copy-start | bytes 1540
  220.3 159.4 %all-gather.5.cloned.1.call-start = ((), (), s32[]{:S(2)}) async-start(), calls=%async_computation.4 | async-start | bytes 2228224 | tf_op jit(solution)/shard_map/all_gather | solution.py:75
  317.2 184.6 %reduce-scatter.5.cloned.1.call-start = ((), (), s32[]{:S(2)}) async-start(), calls=%async_computation.5 | async-start | bytes 2228224 | tf_op jit(solution)/shard_map/reduce_scatter | solution.py:92
  414.6 86.0 %copy-start.2 = (f32[256,128]{1,0:T(8,128)S(1)}, f32[256,128]{1,0:T(8,128)}, u32[]{:S(2)}) copy-start(f32[256,128]{1,0:T(8,128)} %reduce-scatter.3.cloned.1.call-done) | copy-start | bytes 393220
  424.0 332.2 %all-reduce.4.cloned.1.call-start = ((), (), s32[]{:S(2)}) async-start(), calls=%async_computation.6 | async-start | bytes 131072 | tf_op jit(solution)/shard_map/psum | solution.py:74
Sparse Core Ops, SparseCore 0:
  85.1 89.0 all-gather.2
  220.5 93.7 reduce-scatter.2
  317.5 62.1 all-gather.4
  424.1 77.1 reduce-scatter.4
  507.3 248.8 all-reduce.3
where the time goes:
time: 765 us; the launch traced here: 764 us
  waiting for transfers between devices  409 us (53%)
  blocking collectives  232 us (30%)
  matrix products  59 us (8%)
  local copies, waits for them, and re-layouts  38.9 us (5%)
  between operations  15.9 us (2%)
  other arithmetic  8.34 us (1%)
    psum x1, waiting for transfers between devices, local(): weight_grad, bias_grad = lax.psum((weight_part, bias_part), ('row', 'col'))  253 us
    unnamed x2, blocking collectives  156 us
    all_gather x1, waiting for transfers between devices, local(): gathered = lax.all_gather(scaled, 'row', axis=0, tiled=True)  89.2 us
    psum x1, blocking collectives, local(): weight_grad, bias_grad = lax.psum((weight_part, bias_part), ('row', 'col'))  76.6 us
    all_gather x1, waiting for transfers between devices, local(): lax.all_gather(back_rows * dst_scale[:, None], 'col', axis=0, tiled=True)  62.5 us
    dot_general x1, matrix products, local(): jnp.einsum('kab,kbh->kah', adjacency, taken, precision=lax.Precision.HIGH...  21.5 us
    dot_general x1, matrix products, local(): jnp.einsum('kab,kah->kbh', adjacency, taken_back, precision=lax.Precision...  19.7 us
  transfers between devices with their start and end apart: 5, of which 4 were waited for; matrix products, arithmetic and copies ran while one was open for 0% of the time, Pallas kernels for 0%

commit v1 on v0

--- a/solution.py
+++ b/solution.py
@@ -4,6 +4,10 @@
 from jax.sharding import PartitionSpec as P
 
 TILE = 128
+
+
+def read_packet(own_rows):
+    return jax.lax.psum(jax.lax.psum(own_rows, axis_name="row"), axis_name="col")
 
 
 def dense_step(aggregated, weight, bias_vector, cotangent):
@@ -71,7 +75,7 @@
     activated, weight_part, bias_part, back_rows = dense_step(
         aggregated, weight, bias_vector, out_grad
     )
-    weight_grad, bias_grad = lax.psum((weight_part, bias_part), ("row", "col"))
+    weight_grad, bias_grad = read_packet((weight_part, bias_part))
     row_grads = lax.all_gather(back_rows * dst_scale[:, None], "col", axis=0, tiled=True)
     taken_back = jnp.take(row_grads.reshape(tile_rows, TILE, width), tile_row, axis=0)
     product_back = jnp.einsum(

time: 765 us -> 794 us (1.038)
  waiting for transfers between devices: 409 us -> 431 us
    reduce_scatter x1, waiting for transfers between devices: 0.02 us -> 90.8 us  [local(): lax.psum_scatter(partial_back, 'row', scatter_dimension=0, tiled=True)]
    psum x1 -> x2, waiting for transfers between devices: 253 us -> 185 us  [the longest x1 174 us: read_packet(): jax.lax.psum(jax.lax.psum(own_rows, axis_name='row'), axis_name='col')]
    psum x1 -> x2, blocking collectives: 76.6 us -> 82.9 us  [the longest x1 49.6 us: read_packet(): jax.lax.psum(jax.lax.psum(own_rows, axis_name='row'), axis_name='col')]
  transfers between devices with their start and end apart: 5 -> 6, of which waited for: 4 -> 6; matrix products, arithmetic and copies ran while one was open for 0% -> 6% of each run, Pallas kernels for 0% -> 0%
where the time goes in v1:
time: 794 us; the launch traced here: 793 us
  waiting for transfers between devices  431 us (54%)
  blocking collectives  239 us (30%)
  matrix products  59.9 us (8%)
  local copies, waits for them, and re-layouts  38.9 us (5%)
  between operations  16.2 us (2%)
  other arithmetic  8.34 us (1%)
    psum x1, waiting for transfers between devices, read_packet(): jax.lax.psum(jax.lax.psum(own_rows, axis_name='row'), axis_name='col')  174 us
    unnamed x2, blocking collectives  156 us
    reduce_scatter x1, waiting for transfers between devices, local(): lax.psum_scatter(partial_back, 'row', scatter_dimension=0, tiled=True)  90.8 us
    all_gather x1, waiting for transfers between devices, local(): gathered = lax.all_gather(scaled, 'row', axis=0, tiled=True)  89.2 us
    all_gather x1, waiting for transfers between devices, local(): lax.all_gather(back_rows * dst_scale[:, None], 'col', axis=0, tiled=True)  60 us
    psum x1, blocking collectives, read_packet(): jax.lax.psum(jax.lax.psum(own_rows, axis_name='row'), axis_name='col')  49.6 us
    psum x1, blocking collectives, read_packet(): jax.lax.psum(own_rows, axis_name='row')  33.3 us
    dot_general x1, matrix products, local(): jnp.einsum('kab,kbh->kah', adjacency, taken, precision=lax.Precision.HIGH...  21.5 us
  transfers between devices with their start and end apart: 6, of which 6 were waited for; matrix products, arithmetic and copies ran while one was open for 6% of the time, Pallas kernels for 0%

profile of v1, /device:TPU:1, one launch (start us, length us, event | category | flops | bytes accessed | tf_op | source)
XLA Modules:
  0.0 793.1 jit_solution(15905517699055009396)
XLA Ops:
  9.9 5.7 convert_reduce_fusion
  15.8 68.3 %all-reduce = f32[4096]{0:T(1024)S(1)} all-reduce(f32[4096]{0:T(1024)S(1)} %convolution_bitcast_fusion.1), channel_id=2, replica_groups=mesh['row'=16,'col'=16] {'row'}, use_global_device_ids=true, to_apply=%region_1.2.clone | all-reduce | flops 4096 | bytes 32768
  85.1 89.2 %all-gather.3.cloned.1.call-done = f32[4096,128]{1,0:T(8,128)} async-done(((f32[256,128]{1,0:T(8,128)}), f32[4096,128]{1,0:T(8,128)}) %all-gather.3.cloned.1.call-update) | async-done | bytes 2097168 | tf_op jit(solution)/shard_map/all_gather | solution.py:53
  174.3 5.9 gather_fusion
  180.1 21.5 %fusion.12 = f32[128,128,128]{1,2,0:T(8,128)} fusion(s32[1,1,128,128,128]{4,3,2,1,0:T(8,128)} %param.13, f32[128,128,128]{2,1,0:T(8,128)} %gather_fusion, pred[128]{0:T(512)(128)(4,1)S(1)} %get-tuple-element.14), kind=kOutput, calls=%fused_computation.16 | convolution fusion | flops 3225419776 | bytes 25165952 | tf_op jit(solution)/shard_map/kab,kbh->kah/dot_general | solution.py:55
  201.7 9.3 %copy.18 = f32[128,128,128]{2,0,1:T(8,128)} copy(f32[128,128,128]{1,2,0:T(8,128)} %fusion.12) | data formatting | bytes 16777216 | tf_op jit(solution)/shard_map/kab,kbh->kah/dot_general | solution.py:55
  211.0 6.8 fusion.30
  217.8 2.6 copy.19
  221.8 87.6 %all-reduce.1 = f32[4096]{0:T(1024)S(1)} all-reduce(f32[4096]{0:T(1024)S(1)} %convolution_bitcast_fusion), channel_id=4, replica_groups=mesh['row'=16,'col'=16] {'col'}, use_global_device_ids=true, to_apply=%region_4.6.clone | all-reduce | flops 4096 | bytes 32768
  309.5 5.2 reduce-scatter.3.cloned.1.call-done
  314.7 1.9 fusion.52
  317.7 2.0 fusion.23
  319.8 60.0 %all-gather.5.cloned.1.call-done = f32[4096,128]{1,0:T(8,128)} async-done(((f32[256,128]{1,0:T(8,128)}), f32[4096,128]{1,0:T(8,128)}) %all-gather.5.cloned.1.call-update) | async-done | bytes 2097168 | tf_op jit(solution)/shard_map/all_gather | solution.py:79
  379.7 5.9 gather_fusion.1
  385.6 19.7 %fusion.17 = f32[128,128,128]{1,2,0:T(8,128)} fusion(s32[1,1,128,128,128]{4,3,2,1,0:T(8,128)} %param.13, f32[128,128,128]{2,1,0:T(8,128)} %gather_fusion.1, pred[128]{0:T(512)(128)(4,1)S(1)} %get-tuple-element.9), kind=kOutput, calls=%fused_computation.17 | convolution fusion | flops 3225419776 | bytes 25165952 | tf_op jit(solution)/shard_map/kab,kah->kbh/dot_general | solution.py:81
  405.4 9.3 %copy.21 = f32[128,128,128]{2,0,1:T(8,128)} copy(f32[128,128,128]{1,2,0:T(8,128)} %fusion.17) | data formatting | bytes 16777216 | tf_op jit(solution)/shard_map/kab,kah->kbh/dot_general | solution.py:81
  414.7 6.7 fusion.31
  421.4 2.6 copy.22
  424.0 33.3 %psum.30 = f32[128]{0:T(128)S(1)} all-reduce(f32[128]{0:T(128)S(1)} %get-tuple-element.7), channel_id=1, replica_groups=mesh['row'=16,'col'=16] {'row'}, use_global_device_ids=true, to_apply=%region_9.11 | all-reduce | flops 128 | bytes 1024 | tf_op jit(solution)/shard_map/psum | solution.py:10
  457.3 49.6 %psum.31 = f32[128]{0:T(128)} all-reduce(f32[128]{0:T(128)S(1)} %psum.30), channel_id=1, replica_groups=mesh['row'=16,'col'=16] {'col'}, use_global_device_ids=true, to_apply=%region_10.12 | all-reduce | flops 128 | bytes 1024 | tf_op jit(solution)/shard_map/psum | solution.py:10
  507.0 11.8 %all-reduce.5.cloned.1.call-done = f32[128,128]{1,0:T(8,128)} async-done(((f32[128,128]{1,0:T(8,128)}), f32[128,128]{1,0:T(8,128)}) %all-reduce.5.cloned.1.call-update) | async-done | bytes 65552 | tf_op jit(solution)/shard_map/psum | solution.py:10
  518.8 90.8 %reduce-scatter.5.cloned.1.call-done = f32[256,128]{1,0:T(8,128)} async-done(((f32[4096,128]{1,0:T(8,128)}), f32[256,128]{1,0:T(8,128)}) %reduce-scatter.5.cloned.1.call-update) | async-done | bytes 131088 | tf_op jit(solution)/shard_map/reduce_scatter | solution.py:96
  609.6 1.7 broadcast_multiply_fusion
  611.3 173.5 %all-reduce.7.cloned.1.call-done = f32[128,128]{1,0:T(8,128)} async-done(((f32[128,128]{1,0:T(8,128)}), f32[128,128]{1,0:T(8,128)}) %all-reduce.7.cloned.1.call-update) | async-done | bytes 65552 | tf_op jit(solution)/shard_map/psum | solution.py:10
  (38 shorter events, 5.9 us)
Async XLA Ops:
  7.2 307.6 %copy-start = (f32[128,128]{1,0:T(8,128)S(1)}, f32[128,128]{1,0:T(8,128)}, u32[]{:S(2)}) copy-start(f32[128,128]{1,0:T(8,128)} %param.10) | copy-start | bytes 196612
  7.2 8.4 %copy-start.2 = (s32[1,1,128]{2,1,0:T(1,128)S(1)}, s32[1,1,128]{2,1,0:T(1,128)}, u32[]{:S(2)}) copy-start(s32[1,1,128]{2,1,0:T(1,128)} %param.14) | copy-start | bytes 1540
  7.2 77.0 %copy-start.1 = (f32[256,128]{1,0:T(8,128)S(1)}, f32[256,128]{1,0:T(8,128)}, u32[]{:S(2)}) copy-start(f32[256,128]{1,0:T(8,128)} %param.9) | copy-start | bytes 393220
  7.2 167.1 %all-gather.3.cloned.1.call-start = ((), (), s32[]{:S(2)}) async-start(), calls=%async_computation.2 | async-start | bytes 2228224 | tf_op jit(solution)/shard_map/all_gather | solution.py:53
  85.0 229.7 %reduce-scatter.3.cloned.1.call-start = ((), (), s32[]{:S(2)}) async-start(), calls=%async_computation.3 | async-start | bytes 2228224 | tf_op jit(solution)/shard_map/reduce_scatter | solution.py:73
  211.0 9.4 %copy-start.5 = (u32[256]{0:T(256)S(1)}, u32[256]{0:T(256)}, u32[]{:S(2)}) copy-start(u32[256]{0:T(256)} %constant.56) | copy-start | bytes 3076
  211.0 103.7 %copy-start.3 = (f32[256,128]{1,0:T(8,128)S(1)}, f32[256,128]{1,0:T(8,128)}, u32[]{:S(2)}) copy-start(f32[256,128]{1,0:T(8,128)} %param.12) | copy-start | bytes 393220
  211.0 103.7 %copy-start.4 = (f32[128]{0:T(128)S(1)}, f32[128]{0:T(128)}, u32[]{:S(2)}) copy-start(f32[128]{0:T(128)} %param.11) | copy-start | bytes 1540
  220.3 159.4 %all-gather.5.cloned.1.call-start = ((), (), s32[]{:S(2)}) async-start(), calls=%async_computation.4 | async-start | bytes 2228224 | tf_op jit(solution)/shard_map/all_gather | solution.py:79
  317.6 201.1 %all-reduce.5.cloned.1.call-start = ((), (), s32[]{:S(2)}) async-start(), calls=%async_computation.6 | async-start | bytes 131072 | tf_op jit(solution)/shard_map/psum | solution.py:10
  319.7 289.9 %reduce-scatter.5.cloned.1.call-start = ((), (), s32[]{:S(2)}) async-start(), calls=%async_computation.5 | async-start | bytes 2228224 | tf_op jit(solution)/shard_map/reduce_scatter | solution.py:96
  424.0 360.8 %all-reduce.7.cloned.1.call-start = ((), (), s32[]{:S(2)}) async-start(), calls=%async_computation.7 | async-start | bytes 131072 | tf_op jit(solution)/shard_map/psum | solution.py:10
Sparse Core Ops, SparseCore 0:
  85.1 89.0 all-gather.2
  220.5 94.2 reduce-scatter.2
  318.0 61.7 all-gather.4
  382.8 135.8 all-reduce.4
  521.1 88.4 reduce-scatter.4
  612.1 172.6 all-reduce.6
